TPU v7x, 32 devices: a whole 2x2x4 slice. The times are simulated.
32 devices in a mesh: grp: 8 (over z, x), dev: 4 (over y, core).
Axes of the slice: x: 2, y: 2, z: 4, core: 2. Of those that a mesh axis runs over, the one named last changes fastest.
Arguments:
- node_src: bfloat16 [4096, 1024], P(('grp', 'dev'))
- hub_feat: bfloat16 [4096, 1024], P(('grp', 'dev'))
- w_query: bfloat16 [1024, 1024], replicated, may hold values from -0.1875 to 0.1875
- w_key: bfloat16 [1024, 1024], replicated, may hold values from -0.1875 to 0.1875
- w_value: bfloat16 [1024, 1024], replicated, may hold values from -0.1875 to 0.1875
- w_out: bfloat16 [1024, 1024], replicated, may hold values from -0.75 to 0.75
- w_att: bfloat16 [16, 16, 64, 64], replicated, may hold values from -0.75 to 0.75
- w_msg: bfloat16 [16, 16, 64, 64], replicated, may hold values from -0.75 to 0.75
- relation_prior: float32 [16, 16], replicated, may hold values from 0.5 to 2
- block_src: int32 [32, 40], P(('grp', 'dev')), may hold values from 0 to 7
- block_dst: int32 [32, 40], P(('grp', 'dev')), may hold values from 0 to 3
- block_type: int32 [32, 40], P(('grp', 'dev')), may hold values from 0 to 15
- block_count: int32 [32], P(('grp', 'dev')), may hold values from 20 to 40, as said below
Outputs:
- hub_out: bfloat16 [4096, 1024], P(('grp', 'dev'))
Inputs may be any that keep to these rules, and one draw needn't show every extreme that they name: `block_count`: some device uses all 40 slots; every hub tile of a group is the target of some used block of that group.
All inputs are finite; a program needn't handle non-finite values.
Results may differ from a plain program's by a relative error of at most 0.018.
The roundings to bfloat16 on the way count: a program that leaves them out, or rounds other values in their place, can miss the bound.
Values may be sent and summed in bfloat16 or wider, within the bound.
No kernel may reach another device: no remote copies, remote signals or barrier semaphores. Data moves between devices by JAX's collectives and lax.ppermute only.
A program may use at most 128 MiB of HBM per device.

v0:
```python
import jax
import jax.numpy as jnp
from jax import lax
from jax.sharding import PartitionSpec as P


def body(
    node_src,
    hub_feat,
    w_query,
    w_key,
    w_value,
    w_out,
    w_att,
    w_msg,
    relation_prior,
    block_src,
    block_dst,
    block_type,
    block_count,
):
    owners = lax.axis_size("dev")
    tile_rows = hub_feat.shape[0]
    width = hub_feat.shape[1]
    heads = relation_prior.shape[1]
    head_dim = width // heads
    group_hubs = owners * tile_rows
    queries = jnp.dot(hub_feat, w_query, preferred_element_type=jnp.float32).astype(jnp.bfloat16)
    all_queries = lax.all_gather(queries, "dev", axis=0, tiled=True)
    w_both = jnp.concatenate([w_key, w_value], axis=1)
    own_kv = jnp.dot(node_src, w_both, preferred_element_type=jnp.float32).astype(jnp.bfloat16)
    keyval = lax.all_gather(own_kv, "grp", axis=0, tiled=True)
    scale_root = jnp.sqrt(jnp.float32(head_dim))

    def one_block(slot, carry):
        highest, denom, total = carry
        src_tile = block_src[0, slot]
        dst_tile = block_dst[0, slot]
        rtype = block_type[0, slot]
        src_rows = lax.dynamic_slice_in_dim(keyval, src_tile * tile_rows, tile_rows, 0)
        keys = src_rows[:, :width].reshape(tile_rows, heads, head_dim)
        values = src_rows[:, width:].reshape(tile_rows, heads, head_dim)
        key_rel = jnp.einsum(
            "shd,hde->she", keys, w_att[rtype], preferred_element_type=jnp.float32
        ).astype(jnp.bfloat16)
        message = jnp.einsum(
            "shd,hde->she", values, w_msg[rtype], preferred_element_type=jnp.float32
        ).astype(jnp.bfloat16)
        start = dst_tile * tile_rows
        tile_q = lax.dynamic_slice_in_dim(all_queries, start, tile_rows, 0).reshape(
            tile_rows, heads, head_dim
        )
        scores = jnp.einsum("thd,shd->hts", tile_q, key_rel, preferred_element_type=jnp.float32)
        scores = scores * (relation_prior[rtype] / scale_root)[:, None, None]
        old_top = lax.dynamic_slice_in_dim(highest, start, tile_rows, 0)
        new_top = jnp.maximum(old_top, scores.max(axis=2).T)
        factor = jnp.exp(old_top - new_top)
        weight = jnp.exp(scores - new_top.T[:, :, None])
        summed = jnp.einsum(
            "hts,she->the", weight.astype(jnp.bfloat16), message, preferred_element_type=jnp.float32
        ).reshape(tile_rows, width)
        old_d = lax.dynamic_slice_in_dim(denom, start, tile_rows, 0)
        old_t = lax.dynamic_slice_in_dim(total, start, tile_rows, 0)
        highest = lax.dynamic_update_slice_in_dim(highest, new_top, start, 0)
        denom = lax.dynamic_update_slice_in_dim(
            denom, old_d * factor + weight.sum(axis=2).T, start, 0
        )
        total = lax.dynamic_update_slice_in_dim(
            total, old_t * jnp.repeat(factor, head_dim, axis=1) + summed, start, 0
        )
        return (highest, denom, total)

    init = (
        jnp.full((group_hubs, heads), -1e30, jnp.float32),
        jnp.zeros((group_hubs, heads), jnp.float32),
        jnp.zeros((group_hubs, width), jnp.float32),
    )
    highest, denom, total = lax.fori_loop(0, block_count[0], one_block, init)
    overall = lax.pmax(highest.astype(jnp.bfloat16), "dev").astype(highest.dtype)
    factor = jnp.exp(highest - overall)
    own_total, own_denom = (
        lax.psum_scatter(
            (total * jnp.repeat(factor, head_dim, axis=1)).astype(jnp.bfloat16),
            "dev",
            scatter_dimension=0,
            tiled=True,
        ).astype(jnp.float32),
        lax.psum_scatter(
            (denom * factor).astype(jnp.bfloat16), "dev", scatter_dimension=0, tiled=True
        ).astype(jnp.float32),
    )
    aggregate = (own_total / jnp.repeat(own_denom, head_dim, axis=1)).astype(jnp.bfloat16)
    return jnp.dot(aggregate, w_out, preferred_element_type=jnp.float32).astype(jnp.bfloat16)


def solution(mesh):
    placed = (
        P(("grp", "dev"), None),
        P(("grp", "dev"), None),
        P(),
        P(),
        P(),
        P(),
        P(),
        P(),
        P(),
        P(("grp", "dev"), None),
        P(("grp", "dev"), None),
        P(("grp", "dev"), None),
        P(("grp", "dev")),
    )
    return jax.shard_map(
        body, mesh=mesh, in_specs=placed, out_specs=P(("grp", "dev"), None), check_vma=False
    )
```

profile of v0, /device:TPU:0, one launch (start us, length us, event | category | flops | bytes accessed | tf_op | source)
XLA Modules:
  0.0 891.4 jit_solution(7226197442229210296)
XLA Ops:
  10.3 4.4 fusion.30
  14.7 15.1 %all-gather.3.cloned.1.call-done = bf16[512,1024]{1,0:T(8,128)(2,1)} async-done(((bf16[128,1024]{1,0:T(8,128)(2,1)}), bf16[512,1024]{1,0:T(8,128)(2,1)}) %all-gather.3.cloned.1.call-update) | async-done | bytes 1048592 | tf_op jit(solution)/shard_map/all_gather | solution.py:29
  29.8 77.1 %all-gather.5.cloned.1.call-done = bf16[1024,2048]{0,1:T(8,128)(2,1)} async-done(((bf16[128,2048]{0,1:T(8,128)(2,1)}), bf16[1024,2048]{0,1:T(8,128)(2,1)}) %all-gather.5.cloned.1.call-update) | async-done | bytes 4194320 | tf_op jit(solution)/shard_map/all_gather | solution.py:32
  108.5 501.4 %while.14 = (s32[]{:T(128)}, f32[512,16]{0,1:T(8,128)S(1)}, f32[512,16]{0,1:T(8,128)S(1)}, f32[512,1024]{0,1:T(8,128)}, s32[]{:T(128)}, /*index=5*/s32[1,40]{1,0...) while((s32[]{:T(128)}, f32[512,16]{0,1:T(8,128)S(1)}, ...), condition=%wide.region_3.0_spmd, body=%wide.region_0.0_spmd.sunk | while | flops 102766624 | bytes 8774229 | solution.py:78
  122.1 2.2 fusion.77
  140.0 2.2 fusion.77
  157.8 2.2 fusion.77
  175.7 2.2 fusion.77
  193.6 2.2 fusion.77
  211.5 2.2 fusion.77
  229.4 2.2 fusion.77
  247.2 2.2 fusion.77
  265.1 2.2 fusion.77
  283.0 2.2 fusion.77
  300.9 2.2 fusion.77
  318.8 2.2 fusion.77
  336.7 2.2 fusion.77
  354.6 2.2 fusion.77
  372.5 2.2 fusion.77
  390.4 2.2 fusion.77
  408.2 2.2 fusion.77
  426.1 2.2 fusion.77
  444.0 2.2 fusion.77
  461.9 2.2 fusion.77
  479.8 2.2 fusion.77
  497.7 2.2 fusion.77
  515.6 2.2 fusion.77
  569.2 2.2 fusion.77
  610.0 10.1 %pmax.7 = bf16[512,16]{0,1:T(8,128)(2,1)S(1)} all-reduce(bf16[512,16]{0,1:T(8,128)(2,1)S(1)} %convert_element_type.51), channel_id=1, replica_groups=mesh['grp'=8,'dev'=4] {'dev'}, use_global_device_ids=true, to_apply=%region_4.0 | all-reduce | flops 8192 | bytes 32768 | tf_op jit(solution)/shard_map/pmax | solution.py:79
  624.2 229.2 %reduce-scatter.9.cloned.1.call-done = bf16[128,16]{1,0:T(8,128)(2,1)} async-done(((bf16[512,16]{1,0:T(8,128)(2,1)}), bf16[128,16]{1,0:T(8,128)(2,1)}) %reduce-scatter.9.cloned.1.call-update) | async-done | bytes 4112
  854.2 26.7 %reduce-scatter.7.cloned.1.call-done = bf16[128,1024]{1,0:T(8,128)(2,1)} async-done(((bf16[512,1024]{1,0:T(8,128)(2,1)}), bf16[128,1024]{1,0:T(8,128)(2,1)}) %reduce-scatter.7.cloned.1.call-update) | async-done | bytes 262160
  882.1 2.8 convolution_convert_fusion.2
  (343 shorter events, 284.6 us)
Async XLA Ops:
  6.5 1.6 copy-start
  6.5 3.8 copy-start.3
  6.5 23.3 %all-gather.3.cloned.1.call-start = ((), (), s32[]{:S(2)}) async-start(), calls=%async_computation.2 | async-start | bytes 1310720 | tf_op jit(solution)/shard_map/all_gather | solution.py:29
  10.3 96.7 %all-gather.5.cloned.1.call-start = ((), (), s32[]{:S(2)}) async-start(), calls=%async_computation.3 | async-start | bytes 4718592 | tf_op jit(solution)/shard_map/all_gather | solution.py:32
  14.7 93.9 %copy-start.1 = (s32[1,40]{1,0:T(1,128)S(1)}, s32[1,40]{1,0:T(1,128)}, u32[]{:S(2)}) copy-start(s32[1,40]{1,0:T(1,128)} %param.25) | copy-start | bytes 484
  14.7 93.9 %copy-start.2 = (s32[1,40]{1,0:T(1,128)S(1)}, s32[1,40]{1,0:T(1,128)}, u32[]{:S(2)}) copy-start(s32[1,40]{1,0:T(1,128)} %param.26) | copy-start | bytes 484
  14.7 93.9 %copy-start.4 = (s32[1,40]{1,0:T(1,128)S(1)}, s32[1,40]{1,0:T(1,128)}, u32[]{:S(2)}) copy-start(s32[1,40]{1,0:T(1,128)} %param.24) | copy-start | bytes 484
  14.7 838.7 %reduce-scatter.9.cloned.1.call-start = ((), (), s32[]{:S(2)}) async-start(), calls=%async_computation.5 | async-start | bytes 163840
  620.9 259.9 %reduce-scatter.7.cloned.1.call-start = ((), (), s32[]{:S(2)}) async-start(), calls=%async_computation.4 | async-start | bytes 1310720
Sparse Core Ops, SparseCore 0:
  10.4 19.4 all-gather.2
  31.9 75.0 all-gather.4
  621.0 232.2 reduce-scatter.8
  855.9 24.8 reduce-scatter.6
where the time goes:
time: 902 us; the launch traced here: 891 us
  waiting for transfers between devices  348 us (39%)
  loops' own time  176 us (20%)
  other arithmetic  119 us (13%)
  matrix products  117 us (13%)
  local copies, waits for them, and re-layouts  107 us (12%)
  between operations  13.2 us (1%)
  blocking collectives  10.1 us (1%)
    unnamed x6, waiting for transfers between devices  256 us
    another operation x1, loops' own time, body(): highest, denom, total = lax.fori_loop(0, block_count[0], one_block, init)  176 us
    all_gather x1, waiting for transfers between devices, body(): keyval = lax.all_gather(own_kv, 'grp', axis=0, tiled=True)  77.1 us
    dot_general x28, matrix products, one_block(): jnp.einsum('hts,she->the', weight.astype(jnp.bfloat16), message, preferre...  61.1 us
    dynamic_update_slice x28, other arithmetic, one_block(): lax.dynamic_update_slice_in_dim(total, old_t * jnp.repeat(factor, head_di...  59.6 us
    dynamic_slice x56, local copies, waits for them, and re-layouts, one_block(): lax.dynamic_slice_in_dim(all_queries, start, tile_rows, 0)  50.6 us
    slice x28, local copies, waits for them, and re-layouts, one_block(): values = src_rows[:, width:].reshape(tile_rows, heads, head_dim)  49.5 us
    dot_general x28, matrix products, one_block(): jnp.einsum('thd,shd->hts', tile_q, key_rel, preferred_element_type=jnp.fl...  46.9 us
  transfers between devices with their start and end apart: 4, of which 4 were waited for; matrix products, arithmetic and copies ran while one was open for 1% of the time, Pallas kernels for 0%

commit v1 on v0

--- a/solution.py
+++ b/solution.py
@@ -2,6 +2,13 @@
 import jax.numpy as jnp
 from jax import lax
 from jax.sharding import PartitionSpec as P
+
+
+def play_pages(my_tile, out_dim):
+    x_new = list(my_tile.shape[1:])
+    x_new[out_dim] *= my_tile.shape[0]
+    found_now = jnp.moveaxis(my_tile, 0, out_dim).reshape(x_new)
+    return found_now
 
 
 def body(
@@ -29,7 +36,23 @@
     all_queries = lax.all_gather(queries, "dev", axis=0, tiled=True)
     w_both = jnp.concatenate([w_key, w_value], axis=1)
     own_kv = jnp.dot(node_src, w_both, preferred_element_type=jnp.float32).astype(jnp.bfloat16)
-    keyval = lax.all_gather(own_kv, "grp", axis=0, tiled=True)
+    p_count = lax.axis_size("grp")
+    rack = [(h, (h + 1) % p_count) for h in range(p_count)]
+    u_next, n_now = ([], [])
+    runs = [(tick, p) for p, tick in rack]
+    for to_i in [*range(p_count - 1)]:
+        if to_i % 2 == 0:
+            long_array = lax.ppermute(u_next[-1] if u_next else own_kv, axis_name="grp", perm=rack)
+            u_next.append(long_array)
+        else:
+            current_arr = lax.ppermute(n_now[-1] if n_now else own_kv, axis_name="grp", perm=runs)
+            n_now.append(current_arr)
+    e_now = jnp.stack([*u_next[::-1], own_kv, *n_now], axis=0)
+    row_out = len(u_next)
+    answer = lax.axis_index("grp")
+    k_now = answer - row_out
+    e_now = e_now[(jnp.arange(p_count) - k_now) % p_count]
+    keyval = play_pages(e_now, 0)
     scale_root = jnp.sqrt(jnp.float32(head_dim))
 
     def one_block(slot, carry):

time: 902 us -> 982 us (1.089)
  local copies, waits for them, and re-layouts: 107 us -> 166 us
  starting transfers between devices: 0.13 us -> 37.6 us
  waiting for transfers between devices: 348 us -> 320 us
  loops' own time: 176 us -> 188 us
    all_gather x1 -> x0, waiting for transfers between devices: 77.1 us -> none  [body(): keyval = lax.all_gather(own_kv, 'grp', axis=0, tiled=True)]
    while x0 -> x56, local copies, waits for them, and re-layouts: none -> 54.7 us
    ppermute x0 -> x7, waiting for transfers between devices: none -> 48.7 us  [the longest x4 48.7 us: body(): lax.ppermute(u_next[-1] if u_next else own_kv, axis_name='grp', perm=rack)]
    ppermute x0 -> x7, starting transfers between devices: none -> 37.5 us  [the longest x3 29.4 us: body(): lax.ppermute(n_now[-1] if n_now else own_kv, axis_name='grp', perm=runs)]
    dynamic_slice x56, local copies, waits for them, and re-layouts: 50.6 us -> 32 us  [one_block(): lax.dynamic_slice_in_dim(all_queries, start, tile_rows, 0)]
    unnamed x6 -> x5, waiting for transfers between devices: 256 us -> 272 us
    all_gather x1, waiting for transfers between devices: 15.1 us -> 0.01 us  [body(): all_queries = lax.all_gather(queries, 'dev', axis=0, tiled=True)]
    another operation x1, loops' own time: 176 us -> 188 us  [body(): highest, denom, total = lax.fori_loop(0, block_count[0], one_block, init)]
  transfers between devices with their start and end apart: 4 -> 10, of which waited for: 4 -> 6; matrix products, arithmetic and copies ran while one was open for 1% -> 3% of each run, Pallas kernels for 0% -> 0%
where the time goes in v1:
time: 982 us; the launch traced here: 970 us
  waiting for transfers between devices  320 us (33%)
  loops' own time  188 us (19%)
  local copies, waits for them, and re-layouts  166 us (17%)
  other arithmetic  122 us (12%)
  matrix products  114 us (12%)
  starting transfers between devices  37.6 us (4%)
  between operations  13.2 us (1%)
  blocking collectives  10.1 us (1%)
    unnamed x5, waiting for transfers between devices  272 us
    another operation x1, loops' own time, body(): highest, denom, total = lax.fori_loop(0, block_count[0], one_block, init)  188 us
    dot_general x28, matrix products, one_block(): jnp.einsum('hts,she->the', weight.astype(jnp.bfloat16), message, preferre...  61.5 us
    dynamic_update_slice x28, other arithmetic, one_block(): lax.dynamic_update_slice_in_dim(total, old_t * jnp.repeat(factor, head_di...  59.9 us
    while x56, local copies, waits for them, and re-layouts  54.7 us
    slice x28, local copies, waits for them, and re-layouts, one_block(): values = src_rows[:, width:].reshape(tile_rows, heads, head_dim)  49.6 us
    ppermute x4, waiting for transfers between devices, body(): lax.ppermute(u_next[-1] if u_next else own_kv, axis_name='grp', perm=rack)  48.7 us
    dot_general x28, matrix products, one_block(): jnp.einsum('thd,shd->hts', tile_q, key_rel, preferred_element_type=jnp.fl...  44.7 us
  transfers between devices with their start and end apart: 10, of which 6 were waited for; matrix products, arithmetic and copies ran while one was open for 3% of the time, Pallas kernels for 0%

profile of v1, /device:TPU:0, one launch (start us, length us, event | category | flops | bytes accessed | tf_op | source)
XLA Modules:
  0.0 970.2 jit_solution(3539189784006678236)
XLA Ops:
  6.5 3.7 fusion.27
  10.2 3.0 collective-permute-start
  13.2 15.0 %collective-permute-done = bf16[128,2048]{0,1:T(8,128)(2,1)S(1)} collective-permute-done((bf16[128,2048]{0,1:T(8,128)(2,1)S(1)}, bf16[128,2048]{0,1:T(8,128)(2,1)S(1)}, u32[]{:S(2)}, u32[]{:S(2)}) %collective-permute-start) | collective-permute-done | bytes 524320 | tf_op jit(solution)/shard_map/ppermute | solution.py:45
  28.2 4.7 collective-permute-start.4
  32.9 17.4 %collective-permute-done.1 = bf16[128,2048]{0,1:T(8,128)(2,1)S(1)} collective-permute-done((bf16[128,2048]{0,1:T(8,128)(2,1)S(1)}, bf16[128,2048]{0,1:T(8,128)(2,1)S(1)}, u32[]{:S(2)}, u32[]{:S(2)}) %collective-permute-start.1) | collective-permute-done | bytes 524320 | tf_op jit(solution)/shard_map/ppermute | solution.py:45
  50.3 2.5 collective-permute-start.2
  52.8 12.2 %collective-permute-start.5 = (bf16[128,2048]{0,1:T(8,128)(2,1)}, bf16[128,2048]{0,1:T(8,128)(2,1)}, u32[]{:S(2)}, u32[]{:S(2)}) collective-permute-start(bf16[128,2048]{0,1:T(8,128)(2,1)} %collective-permute-done.4), channel_id=1, source_target_pairs={{4,0},{8,4},{12,8},{16,12},{20,16},{24,20},{28,24},{0,28},{5,1},{9... | collective-permute-start | bytes 1572872 | tf_op jit(solution)/shard_map/ppermute | solution.py:48
  65.0 9.1 collective-permute-done.2
  74.2 2.6 collective-permute-start.3
  78.0 12.5 %collective-permute-start.6 = (bf16[128,2048]{0,1:T(8,128)(2,1)}, bf16[128,2048]{0,1:T(8,128)(2,1)S(1)}, u32[]{:S(2)}, u32[]{:S(2)}) collective-permute-start(bf16[128,2048]{0,1:T(8,128)(2,1)} %collective-permute-done.5), channel_id=1, source_target_pairs={{4,0},{8,4},{12,8},{16,12},{20,16},{24,20},{28,24},{0,28},{5,1},{9... | collective-permute-start | bytes 1572872 | tf_op jit(solution)/shard_map/ppermute | solution.py:48
  90.5 7.1 collective-permute-done.3
  109.6 5.2 gather_fusion
  114.8 6.5 copy.21
  123.0 550.2 %while.14 = (s32[]{:T(128)}, f32[512,16]{0,1:T(8,128)S(1)}, f32[512,16]{0,1:T(8,128)S(1)}, f32[512,1024]{0,1:T(8,128)}, s32[]{:T(128)}, /*index=5*/s32[1,40]{1,0...) while((s32[]{:T(128)}, f32[512,16]{0,1:T(8,128)S(1)}, ...), condition=%wide.region_3.4_spmd, body=%wide.region_0.3_spmd.sunk | while | flops 102766624 | bytes 9822797 | solution.py:101
  138.1 2.2 fusion.76
  157.7 2.2 fusion.76
  177.3 2.2 fusion.76
  216.6 2.2 fusion.76
  275.4 2.2 fusion.76
  295.1 2.2 fusion.76
  314.7 2.2 fusion.76
  354.0 2.2 fusion.76
  412.9 2.2 fusion.76
  452.1 2.2 fusion.76
  471.7 2.2 fusion.76
  530.6 2.2 fusion.76
  589.5 2.2 fusion.76
  648.3 2.2 fusion.76
  673.2 10.1 %pmax.7 = bf16[512,16]{0,1:T(8,128)(2,1)S(1)} all-reduce(bf16[512,16]{0,1:T(8,128)(2,1)S(1)} %convert_element_type.51), channel_id=1, replica_groups=mesh['grp'=8,'dev'=4] {'dev'}, use_global_device_ids=true, to_apply=%region_4.5 | all-reduce | flops 8192 | bytes 32768 | tf_op jit(solution)/shard_map/pmax | solution.py:102
  687.4 244.7 %reduce-scatter.9.cloned.1.call-done = bf16[128,16]{1,0:T(8,128)(2,1)} async-done(((bf16[512,16]{1,0:T(8,128)(2,1)}), bf16[128,16]{1,0:T(8,128)(2,1)}) %reduce-scatter.9.cloned.1.call-update) | async-done | bytes 4112
  932.9 26.8 %reduce-scatter.7.cloned.1.call-done = bf16[128,1024]{1,0:T(8,128)(2,1)} async-done(((bf16[512,1024]{1,0:T(8,128)(2,1)}), bf16[128,1024]{1,0:T(8,128)(2,1)}) %reduce-scatter.7.cloned.1.call-update) | async-done | bytes 262160
  960.9 2.8 convolution_convert_fusion.2
  (424 shorter events, 352.4 us)
Async XLA Ops:
  6.5 70.2 %copy-start = (bf16[1024,1024]{1,0:T(8,128)(2,1)S(1)}, bf16[1024,1024]{1,0:T(8,128)(2,1)}, u32[]{:S(2)}) copy-start(bf16[1024,1024]{1,0:T(8,128)(2,1)} %param.17) | copy-start | bytes 6291460
  6.5 70.2 %copy-start.2 = (bf16[128,1024]{1,0:T(8,128)(2,1)S(1)}, bf16[128,1024]{1,0:T(8,128)(2,1)}, u32[]{:S(2)}) copy-start(bf16[128,1024]{1,0:T(8,128)(2,1)} %param.16) | copy-start | bytes 786436
  6.5 114.8 %all-gather.2.cloned.1.call-start = ((), (), s32[]{:S(2)}) async-start(), calls=%async_computation.2 | async-start | bytes 1310720 | tf_op jit(solution)/shard_map/all_gather | solution.py:36
  10.2 18.0 %collective-permute-start = (bf16[128,2048]{0,1:T(8,128)(2,1)S(1)}, bf16[128,2048]{0,1:T(8,128)(2,1)S(1)}, u32[]{:S(2)}, u32[]{:S(2)}) collective-permute-start(bf16[128,2048]{0,1:T(8,128)(2,1)S(1)} %bitcast.131), channel_id=1, source_target_pairs={{0,4},{4,8},{8,12},{12,16},{16,20},{20,24},{24,28},{28,0},{1,5},{5... | collective-permute-start | bytes 1572872 | tf_op jit(solution)/shard_map/ppermute | solution.py:45
  28.2 22.1 %collective-permute-start.1 = (bf16[128,2048]{0,1:T(8,128)(2,1)S(1)}, bf16[128,2048]{0,1:T(8,128)(2,1)S(1)}, u32[]{:S(2)}, u32[]{:S(2)}) collective-permute-start(bf16[128,2048]{0,1:T(8,128)(2,1)S(1)} %collective-permute-done), channel_id=1, source_target_pairs={{0,4},{4,8},{8,12},{12,16},{16,20},{20,24},{24,28},{28,0},{1,5},{5... | collective-permute-start | bytes 1572872 | tf_op jit(solution)/shard_map/ppermute | solution.py:45
  28.2 24.6 %collective-permute-start.4 = (bf16[128,2048]{0,1:T(8,128)(2,1)S(1)}, bf16[128,2048]{0,1:T(8,128)(2,1)}, u32[]{:S(2)}, u32[]{:S(2)}) collective-permute-start(bf16[128,2048]{0,1:T(8,128)(2,1)S(1)} %bitcast.132), channel_id=1, source_target_pairs={{4,0},{8,4},{12,8},{16,12},{20,16},{24,20},{28,24},{0,28},{5,1},{9... | collective-permute-start | bytes 1572872 | tf_op jit(solution)/shard_map/ppermute | solution.py:48
  50.3 2.5 copy-start.1
  50.3 23.9 %collective-permute-start.2 = (bf16[128,2048]{0,1:T(8,128)(2,1)S(1)}, bf16[128,2048]{0,1:T(8,128)(2,1)}, u32[]{:S(2)}, u32[]{:S(2)}) collective-permute-start(bf16[128,2048]{0,1:T(8,128)(2,1)S(1)} %collective-permute-done.1), channel_id=1, source_target_pairs={{0,4},{4,8},{8,12},{12,16},{16,20},{20,24},{24,28},{28,0},{1,5},{5... | collective-permute-start | bytes 1572872 | tf_op jit(solution)/shard_map/ppermute | solution.py:45
  52.8 25.2 %collective-permute-start.5 = (bf16[128,2048]{0,1:T(8,128)(2,1)}, bf16[128,2048]{0,1:T(8,128)(2,1)}, u32[]{:S(2)}, u32[]{:S(2)}) collective-permute-start(bf16[128,2048]{0,1:T(8,128)(2,1)} %collective-permute-done.4), channel_id=1, source_target_pairs={{4,0},{8,4},{12,8},{16,12},{20,16},{24,20},{28,24},{0,28},{5,1},{9... | collective-permute-start | bytes 1572872 | tf_op jit(solution)/shard_map/ppermute | solution.py:48
  74.2 23.5 %collective-permute-start.3 = (bf16[128,2048]{0,1:T(8,128)(2,1)}, bf16[128,2048]{0,1:T(8,128)(2,1)}, u32[]{:S(2)}, u32[]{:S(2)}) collective-permute-start(bf16[128,2048]{0,1:T(8,128)(2,1)} %collective-permute-done.2), channel_id=1, source_target_pairs={{0,4},{4,8},{8,12},{12,16},{16,20},{20,24},{24,28},{28,0},{1,5},{5... | collective-permute-start | bytes 1572872 | tf_op jit(solution)/shard_map/ppermute | solution.py:45
  78.0 854.1 %reduce-scatter.9.cloned.1.call-start = ((), (), s32[]{:S(2)}) async-start(), calls=%async_computation.4 | async-start | bytes 163840
  78.0 30.7 %collective-permute-start.6 = (bf16[128,2048]{0,1:T(8,128)(2,1)}, bf16[128,2048]{0,1:T(8,128)(2,1)S(1)}, u32[]{:S(2)}, u32[]{:S(2)}) collective-permute-start(bf16[128,2048]{0,1:T(8,128)(2,1)} %collective-permute-done.5), channel_id=1, source_target_pairs={{4,0},{8,4},{12,8},{16,12},{20,16},{24,20},{28,24},{0,28},{5,1},{9... | collective-permute-start | bytes 1572872 | tf_op jit(solution)/shard_map/ppermute | solution.py:48
  114.8 8.1 copy-start.3
  114.8 8.2 copy-start.4
  114.8 8.2 copy-start.5
  684.1 275.6 %reduce-scatter.7.cloned.1.call-start = ((), (), s32[]{:S(2)}) async-start(), calls=%async_computation.3 | async-start | bytes 1310720
Sparse Core Ops, SparseCore 0:
  78.1 15.1 all-gather.1
  684.3 247.8 reduce-scatter.8
  934.8 24.8 reduce-scatter.6
